TPU v7x, 256 devices: a whole 4x4x8 slice. The times are simulated.
256 devices in a mesh: row: 32 (over x, y, core), col: 8 (over z).
Axes of the slice: x: 4, y: 4, z: 8, core: 2. Of those that a mesh axis runs over, the one named last changes fastest.
Arguments:
- block_values: bfloat16 [32, 8, 192, 128, 128], P('row', 'col'), may hold values from -0.0625 to 0.0625
- block_rows: int32 [32, 8, 192], P('row', 'col'), may hold values from 0 to 4095, as said below
- block_cols: int32 [32, 8, 192], P('row', 'col'), may hold values from 0 to 4095, as said below
- block_counts: int32 [32, 8], P('row', 'col'), may hold values from 48 to 192, as said below
- precond: float32 [8, 512, 128, 128], P('col', 'row')
- right_side: float32 [8, 512, 32, 128], P('col', 'row'), may hold values from -6 to 6
Outputs:
- solution: float32 [8, 512, 32, 128], P('col', 'row')
Inputs may be any that keep to these rules, and one draw needn't show every extreme that they name: `block_rows`: the block rows of device (r, c) lie in [c * 512, (c + 1) * 512); positions may repeat; for each j, at most 9 of a device's 192 slots have (row mod 512) // 16 == j, and in every index of col some j has exactly 9 such slots on every device. `block_cols`: every block column q of device (r, c) has (q mod 512) // 16 == r; positions may repeat. `block_counts`: slots at or past a device's count are unused; some device uses all 192 slots.
All inputs are finite; a program needn't handle non-finite values.
Results may differ from a plain program's by a relative error of at most 0.00073.
Values may be sent and summed in bfloat16 or wider, within the bound.
A program may use at most 64 MiB of HBM per device.

v0:
```python
import jax
import jax.numpy as jnp
from jax import lax
from jax.sharding import PartitionSpec as P

ITERS = 3


def apply_blocks(matrix, field):
    return jnp.einsum("poi,pki->pko", matrix, field, precision=lax.Precision.HIGHEST)


def block_terms(vectors, values, col_local):
    gathered = vectors[col_local]
    return jnp.einsum("ski,soi->sko", gathered, values, preferred_element_type=jnp.float32)


def per_device(block_values, block_rows, block_cols, block_counts, precond, right_side):
    owned = right_side.shape[1]
    row_devices = lax.axis_size("row")
    group = owned * row_devices
    slot_total = block_values.shape[2]
    values = block_values[0, 0]
    row_local = block_rows[0, 0] % group
    col_global = block_cols[0, 0]
    col_local = col_global // group * owned + col_global % owned
    used = block_counts[0, 0]
    live = jnp.arange(slot_total, dtype=jnp.int32) < used
    inverse = precond[0]
    rhs_own = right_side[0]
    solution = apply_blocks(inverse, rhs_own)
    for step in range(ITERS):
        pieces = lax.all_gather(solution.astype(jnp.bfloat16)[None], "col", axis=1, tiled=True)[0]
        terms = block_terms(pieces, values, col_local)
        terms = jnp.where(live[:, None, None], terms, jnp.zeros_like(terms))
        partial_value = jax.ops.segment_sum(terms, row_local, num_segments=group)
        product = lax.psum_scatter(partial_value, "row", scatter_dimension=0, tiled=True)
        residual = rhs_own - solution - product
        solution = solution + apply_blocks(inverse, residual)
    return solution[None]


def solution(mesh):
    placed = (
        P("row", "col", None, None, None),
        P("row", "col", None),
        P("row", "col", None),
        P("row", "col"),
        P("col", "row", None, None),
        P("col", "row", None, None),
    )
    return jax.shard_map(
        per_device,
        mesh=mesh,
        in_specs=placed,
        out_specs=P("col", "row", None, None),
        check_vma=False,
    )
```

profile of v0, /device:TPU:2, one launch (start us, length us, event | category | flops | bytes accessed | tf_op | source)
XLA Modules:
  0.0 562.6 jit_solution(1981962366836233417)
XLA Ops:
  6.5 0.0 copy-start
  6.5 0.0 all-gather.7.cloned.1.call-start
  6.5 1.2 copy-done
  7.8 3.3 fusion.30
  11.1 0.0 all-gather.7.cloned.1.call-update
  11.1 0.0 reduce-scatter.4.cloned.1.call-start
  11.8 0.7 compare_select_fusion
  12.5 0.7 and_select_fusion.2
  13.2 39.4 %all-gather.7.cloned.1.call-done = bf16[128,32,128]{2,1,0:T(8,128)(2,1)} async-done(((bf16[16,32,128]{2,1,0:T(8,128)(2,1)}), bf16[128,32,128]{2,1,0:T(8,128)(2,1)}) %all-gather.7.cloned.1.call-update) | async-done | bytes 1048592 | tf_op jit(solution)/shard_map/all_gather | solution.py:33
  52.6 2.1 gather_fusion
  54.8 7.9 %fusion.6 = f32[192,32,128]{2,1,0:T(8,128)} fusion(bf16[192,32,128]{2,1,0:T(8,128)(2,1)S(1)} %gather_fusion, bf16[1,1,192,128,128]{4,3,2,1,0:T(8,128)(2,1)} %param.6, pred[192]{0:T(512)(128)(4,1)S(1)} %iota_compare_fusion), kind=kOutput, calls=%fused_computation.12 | convolution fusion | flops 202113024 | bytes 11010240 | tf_op jit(solution)/shard_map/ski,soi->sko/dot_general | solution.py:15
  62.7 4.3 broadcast.156.clone
  67.0 25.8 %scatter_fusion = f32[512,32,128]{2,1,0:T(8,128)} fusion(f32[512,32,128]{2,1,0:T(8,128)} %broadcast.156.clone, s32[192]{0:T(256)S(1)} %bitcast.73, f32[192,32,128]{2,1,0:T(8,128)} %fusion.6), kind=kCustom, calls=%fused_computation.3 | custom fusion | flops 786432 | bytes 9437952 | tf_op jit(solution)/shard_map/scatter-add | solution.py:36
  92.8 0.0 copy-start.1
  92.8 0.0 reduce-scatter.4.cloned.1.call-update
  92.9 0.0 all-gather.9.cloned.1.call-start
  92.9 98.6 %reduce-scatter.4.cloned.1.call-done = f32[16,32,128]{2,1,0:T(8,128)} async-done(((f32[512,32,128]{2,1,0:T(8,128)}), f32[16,32,128]{2,1,0:T(8,128)}) %reduce-scatter.4.cloned.1.call-update) | async-done | bytes 262160 | tf_op jit(solution)/shard_map/reduce_scatter | solution.py:37
  191.5 0.0 copy-done.1
  191.5 3.3 fusion.31
  194.8 0.0 all-gather.9.cloned.1.call-update
  194.8 0.0 reduce-scatter.6.cloned.1.call-start
  194.9 38.2 %all-gather.9.cloned.1.call-done = bf16[128,32,128]{2,1,0:T(8,128)(2,1)} async-done(((bf16[16,32,128]{2,1,0:T(8,128)(2,1)}), bf16[128,32,128]{2,1,0:T(8,128)(2,1)}) %all-gather.9.cloned.1.call-update) | async-done | bytes 1048592 | tf_op jit(solution)/shard_map/all_gather | solution.py:33
  233.1 2.1 gather_fusion.1
  235.2 7.9 %fusion.9 = f32[192,32,128]{2,1,0:T(8,128)} fusion(bf16[192,32,128]{2,1,0:T(8,128)(2,1)S(1)} %gather_fusion.1, bf16[1,1,192,128,128]{4,3,2,1,0:T(8,128)(2,1)} %param.6, pred[192]{0:T(512)(128)(4,1)S(1)} %iota_compare_fusion), kind=kOutput, calls=%fused_computation.13 | convolution fusion | flops 202113024 | bytes 11010240 | tf_op jit(solution)/shard_map/ski,soi->sko/dot_general | solution.py:15
  243.1 4.3 broadcast.156.clone.1
  247.4 25.8 %scatter_fusion.1 = f32[512,32,128]{2,1,0:T(8,128)} fusion(f32[512,32,128]{2,1,0:T(8,128)} %broadcast.156.clone.1, s32[192]{0:T(256)S(1)} %bitcast.74, f32[192,32,128]{2,1,0:T(8,128)} %fusion.9), kind=kCustom, calls=%fused_computation.4 | custom fusion | flops 786432 | bytes 9437952 | tf_op jit(solution)/shard_map/scatter-add | solution.py:36
  273.3 0.0 reduce-scatter.6.cloned.1.call-update
  273.3 0.0 all-gather.11.cloned.1.call-start
  273.4 98.6 %reduce-scatter.6.cloned.1.call-done = f32[16,32,128]{2,1,0:T(8,128)} async-done(((f32[512,32,128]{2,1,0:T(8,128)}), f32[16,32,128]{2,1,0:T(8,128)}) %reduce-scatter.6.cloned.1.call-update) | async-done | bytes 262160 | tf_op jit(solution)/shard_map/reduce_scatter | solution.py:37
  371.9 3.3 fusion.32
  375.3 0.0 all-gather.11.cloned.1.call-update
  375.3 0.2 reduce-scatter.8.cloned.1.call-start
  375.5 38.0 %all-gather.11.cloned.1.call-done = bf16[128,32,128]{2,1,0:T(8,128)(2,1)} async-done(((bf16[16,32,128]{2,1,0:T(8,128)(2,1)}), bf16[128,32,128]{2,1,0:T(8,128)(2,1)}) %all-gather.11.cloned.1.call-update) | async-done | bytes 1048592 | tf_op jit(solution)/shard_map/all_gather | solution.py:33
  413.6 2.1 gather_fusion.2
  415.7 7.9 %fusion.12 = f32[192,32,128]{2,1,0:T(8,128)} fusion(bf16[192,32,128]{2,1,0:T(8,128)(2,1)S(1)} %gather_fusion.2, bf16[1,1,192,128,128]{4,3,2,1,0:T(8,128)(2,1)} %param.6, pred[192]{0:T(512)(128)(4,1)S(1)} %iota_compare_fusion), kind=kOutput, calls=%fused_computation.14 | convolution fusion | flops 202113024 | bytes 11010240 | tf_op jit(solution)/shard_map/ski,soi->sko/dot_general | solution.py:15
  423.6 4.3 broadcast.156
  427.9 25.8 %scatter_fusion.2 = f32[512,32,128]{2,1,0:T(8,128)} fusion(f32[512,32,128]{2,1,0:T(8,128)} %broadcast.156, s32[192]{0:T(256)S(1)} %bitcast.75, f32[192,32,128]{2,1,0:T(8,128)} %fusion.12), kind=kCustom, calls=%fused_computation.5 | custom fusion | flops 786432 | bytes 9437952 | tf_op jit(solution)/shard_map/scatter-add | solution.py:36
  453.7 0.0 reduce-scatter.8.cloned.1.call-update
  453.8 98.6 %reduce-scatter.8.cloned.1.call-done = f32[16,32,128]{2,1,0:T(8,128)} async-done(((f32[512,32,128]{2,1,0:T(8,128)}), f32[16,32,128]{2,1,0:T(8,128)}) %reduce-scatter.8.cloned.1.call-update) | async-done | bytes 262160 | tf_op jit(solution)/shard_map/reduce_scatter | solution.py:37
  552.4 3.4 fusion.15
  (2 shorter events, 0.0 us)
Async XLA Ops:
  6.5 1.2 copy-start
  6.5 46.1 %all-gather.7.cloned.1.call-start = ((), (), s32[]{:S(2)}) async-start(), calls=%async_computation.6 | async-start | bytes 1179648 | tf_op jit(solution)/shard_map/all_gather | solution.py:33
  11.1 180.3 %reduce-scatter.4.cloned.1.call-start = ((), (), s32[]{:S(2)}) async-start(), calls=%async_computation.3 | async-start | bytes 8650752 | tf_op jit(solution)/shard_map/reduce_scatter | solution.py:37
  92.8 98.7 %copy-start.1 = (f32[1,16,32,128]{3,2,1,0:T(8,128)S(1)}, f32[1,16,32,128]{3,2,1,0:T(8,128)}, u32[]{:S(2)}) copy-start(f32[1,16,32,128]{3,2,1,0:T(8,128)} %param.11) | copy-start | bytes 786436
  92.9 140.3 %all-gather.9.cloned.1.call-start = ((), (), s32[]{:S(2)}) async-start(), calls=%async_computation.7 | async-start | bytes 1179648 | tf_op jit(solution)/shard_map/all_gather | solution.py:33
  194.8 177.1 %reduce-scatter.6.cloned.1.call-start = ((), (), s32[]{:S(2)}) async-start(), calls=%async_computation.4 | async-start | bytes 8650752 | tf_op jit(solution)/shard_map/reduce_scatter | solution.py:37
  273.3 140.3 %all-gather.11.cloned.1.call-start = ((), (), s32[]{:S(2)}) async-start(), calls=%async_computation.8 | async-start | bytes 1179648 | tf_op jit(solution)/shard_map/all_gather | solution.py:33
  375.3 177.1 %reduce-scatter.8.cloned.1.call-start = ((), (), s32[]{:S(2)}) async-start(), calls=%async_computation.5 | async-start | bytes 8650752 | tf_op jit(solution)/shard_map/reduce_scatter | solution.py:37
Sparse Core Ops, SparseCore 0:
  11.2 41.3 all-gather.6
  93.0 98.4 reduce-scatter.3
  195.0 38.0 all-gather.8
  273.4 98.4 reduce-scatter.5
  375.4 38.0 all-gather.10
  453.9 98.4 reduce-scatter.7
where the time goes:
time: 564 us; the launch traced here: 563 us
  waiting for transfers between devices  412 us (73%)
  other arithmetic  78.9 us (14%)
  matrix products  37.1 us (7%)
  local copies, waits for them, and re-layouts  20.5 us (4%)
  between operations  14.2 us (3%)
    reduce_scatter x3, waiting for transfers between devices, per_device(): lax.psum_scatter(partial_value, 'row', scatter_dimension=0, tiled=True)  296 us
    all_gather x3, waiting for transfers between devices, per_device(): lax.all_gather(solution.astype(jnp.bfloat16)[None], 'col', axis=1, tiled=...  116 us
    scatter-add x3, other arithmetic, per_device(): partial_value = jax.ops.segment_sum(terms, row_local, num_segments=group)  77.5 us
    dot_general x3, matrix products, block_terms(): jnp.einsum('ski,soi->sko', gathered, values, preferred_element_type=jnp.f...  23.7 us
    dot_general x4, matrix products, apply_blocks(): jnp.einsum('poi,pki->pko', matrix, field, precision=lax.Precision.HIGHEST)  13.4 us
    another operation x3, local copies, waits for them, and re-layouts  12.9 us
  transfers between devices with their start and end apart: 6, of which 6 were waited for; matrix products, arithmetic and copies ran while one was open for 0% of the time, Pallas kernels for 0%

commit v1 on v0

--- a/solution.py
+++ b/solution.py
@@ -1,9 +1,40 @@
+import functools
 import jax
 import jax.numpy as jnp
 from jax import lax
 from jax.sharding import PartitionSpec as P
 
 ITERS = 3
+
+
+def feed_patches(x_part, row_dim):
+    even = list(x_part.shape[1:])
+    even[row_dim] *= x_part.shape[0]
+    return jnp.moveaxis(x_part, 0, row_dim).reshape(even)
+
+
+def move_classes(unit, mesh_ax, at_axis):
+    fan = lax.axis_size(mesh_ax)
+    queue = tuple(((hop_no, (hop_no + 1) % fan) for hop_no in range(fan)))
+    frames = tuple(((jj, q) for q, jj in queue))
+    near, tile_out = ([], [])
+    no = 0
+    while no < fan - 1:
+        if no % 2 == 0:
+            step_out = lax.ppermute(near[-1] if near else unit, mesh_ax, queue)
+            near.append(step_out)
+        else:
+            tile_out.append(lax.ppermute(tile_out[-1] if tile_out else unit, mesh_ax, frames))
+        no = no + 1
+    low = jnp.stack([*near[::-1], unit, *tile_out], axis=0)
+    main = lax.axis_index(mesh_ax)
+    field_out = len(near)
+    current_block = main - field_out
+    low = low[(jnp.arange(fan) - current_block) % fan]
+    return feed_patches(low, at_axis)
+
+
+_put_series = functools.partial(move_classes, mesh_ax="col", at_axis=1)
 
 
 def apply_blocks(matrix, field):
@@ -30,7 +61,7 @@
     rhs_own = right_side[0]
     solution = apply_blocks(inverse, rhs_own)
     for step in range(ITERS):
-        pieces = lax.all_gather(solution.astype(jnp.bfloat16)[None], "col", axis=1, tiled=True)[0]
+        pieces = _put_series(solution.astype(jnp.bfloat16)[None])[0]
         terms = block_terms(pieces, values, col_local)
         terms = jnp.where(live[:, None, None], terms, jnp.zeros_like(terms))
         partial_value = jax.ops.segment_sum(terms, row_local, num_segments=group)

time: 564 us -> 539 us (0.956)
  waiting for transfers between devices: 412 us -> 345 us
  starting transfers between devices: 0.39 us -> 36.1 us
  local copies, waits for them, and re-layouts: 20.5 us -> 27.2 us
    all_gather x3 -> x0, waiting for transfers between devices: 116 us -> none  [per_device(): lax.all_gather(solution.astype(jnp.bfloat16)[None], 'col', axis=1, tiled=...]
    ppermute x0 -> x21, waiting for transfers between devices: none -> 43.3 us  [the longest x12 42.4 us: move_classes(): step_out = lax.ppermute(near[-1] if near else unit, mesh_ax, queue)]
    ppermute x0 -> x21, starting transfers between devices: none -> 36 us  [the longest x9 29.1 us: move_classes(): lax.ppermute(tile_out[-1] if tile_out else unit, mesh_ax, frames)]
    reduce_scatter x3, waiting for transfers between devices: 296 us -> 302 us  [per_device(): lax.psum_scatter(partial_value, 'row', scatter_dimension=0, tiled=True)]
    another operation x3 -> x6, local copies, waits for them, and re-layouts: 12.9 us -> 13 us
  transfers between devices with their start and end apart: 6 -> 24, of which waited for: 6 -> 19; matrix products, arithmetic and copies ran while one was open for 0% -> 0% of each run, Pallas kernels for 0% -> 0%
where the time goes in v1:
time: 539 us; the launch traced here: 538 us
  waiting for transfers between devices  345 us (64%)
  other arithmetic  79.1 us (15%)
  matrix products  36.6 us (7%)
  starting transfers between devices  36.1 us (7%)
  local copies, waits for them, and re-layouts  27.2 us (5%)
  between operations  14.1 us (3%)
    reduce_scatter x3, waiting for transfers between devices, per_device(): lax.psum_scatter(partial_value, 'row', scatter_dimension=0, tiled=True)  302 us
    scatter-add x3, other arithmetic, per_device(): partial_value = jax.ops.segment_sum(terms, row_local, num_segments=group)  77.5 us
    ppermute x12, waiting for transfers between devices, move_classes(): step_out = lax.ppermute(near[-1] if near else unit, mesh_ax, queue)  42.4 us
    ppermute x9, starting transfers between devices, move_classes(): lax.ppermute(tile_out[-1] if tile_out else unit, mesh_ax, frames)  29.1 us
    dot_general x3, matrix products, block_terms(): jnp.einsum('ski,soi->sko', gathered, values, preferred_element_type=jnp.f...  25.2 us
    another operation x3, local copies, waits for them, and re-layouts  12.9 us
    dot_general x4, matrix products, apply_blocks(): jnp.einsum('poi,pki->pko', matrix, field, precision=lax.Precision.HIGHEST)  11.4 us
  transfers between devices with their start and end apart: 24, of which 19 were waited for; matrix products, arithmetic and copies ran while one was open for 0% of the time, Pallas kernels for 0%

profile of v1, /device:TPU:2, one launch (start us, length us, event | category | flops | bytes accessed | tf_op | source)
XLA Modules:
  0.0 538.2 jit_solution(18275011482617165357)
XLA Ops:
  6.5 1.2 copy-done
  7.8 2.7 fusion.19
  10.5 2.0 collective-permute-start
  12.5 4.0 collective-permute-start.4
  17.2 2.7 collective-permute-done
  20.6 5.5 %collective-permute-done.1 = bf16[1,16,32,128]{3,2,1,0:T(8,128)(2,1)S(1)} collective-permute-done((bf16[1,16,32,128]{3,2,1,0:T(8,128)(2,1)S(1)}, bf16[1,16,32,128]{3,2,1,0:T(8,128)(2,1)S(1)}, u32[]{:S(2)}, u32[]{:S(2)}) %collective-permute-start.1) | collective-permute-done | bytes 131104 | tf_op jit(solution)/shard_map/ppermute | solution.py:24
  26.8 3.3 collective-permute-start.5
  30.1 2.2 collective-permute-done.2
  32.6 3.7 collective-permute-start.6
  36.3 2.2 collective-permute-done.3
  39.6 2.0 gather_fusion.1
  41.6 8.4 %fusion.6 = f32[192,32,128]{2,1,0:T(8,128)} fusion(bf16[192,32,128]{2,1,0:T(8,128)(2,1)} %gather_fusion.1, bf16[1,1,192,128,128]{4,3,2,1,0:T(8,128)(2,1)} %param.6, pred[192]{0:T(512)(128)(4,1)S(1)} %iota_compare_fusion), kind=kOutput, calls=%fused_computation.15 | convolution fusion | flops 202113024 | bytes 11010240 | tf_op jit(solution)/shard_map/ski,soi->sko/dot_general | solution.py:46
  50.0 4.3 broadcast.221.clone
  54.3 25.8 %scatter_fusion = f32[512,32,128]{2,1,0:T(8,128)} fusion(f32[512,32,128]{2,1,0:T(8,128)} %broadcast.221.clone, s32[192]{0:T(256)S(1)} %bitcast.129, f32[192,32,128]{2,1,0:T(8,128)} %fusion.6), kind=kCustom, calls=%fused_computation.6 | custom fusion | flops 786432 | bytes 9437952 | tf_op jit(solution)/shard_map/scatter-add | solution.py:67
  80.2 101.2 %reduce-scatter.4.cloned.1.call-done = f32[16,32,128]{2,1,0:T(8,128)} async-done(((f32[512,32,128]{2,1,0:T(8,128)}), f32[16,32,128]{2,1,0:T(8,128)}) %reduce-scatter.4.cloned.1.call-update) | async-done | bytes 262160 | tf_op jit(solution)/shard_map/reduce_scatter | solution.py:68
  181.4 2.7 convolution_add_fusion.2
  184.1 1.8 collective-permute-start.7
  185.9 4.7 collective-permute-done.7
  191.3 2.5 collective-permute-start.11
  193.9 3.4 collective-permute-done.8
  197.4 3.3 collective-permute-start.12
  200.8 3.9 collective-permute-done.9
  204.6 3.2 collective-permute-start.13
  207.9 2.9 collective-permute-done.10
  211.1 1.0 copy-done.2
  212.0 2.0 gather_fusion.2
  214.0 2.0 gather_fusion.3
  216.0 8.4 %fusion.9 = f32[192,32,128]{2,1,0:T(8,128)} fusion(bf16[192,32,128]{2,1,0:T(8,128)(2,1)} %gather_fusion.3, bf16[1,1,192,128,128]{4,3,2,1,0:T(8,128)(2,1)} %param.6, pred[192]{0:T(512)(128)(4,1)S(1)} %iota_compare_fusion), kind=kOutput, calls=%fused_computation.16 | convolution fusion | flops 202113024 | bytes 11010240 | tf_op jit(solution)/shard_map/ski,soi->sko/dot_general | solution.py:46
  224.4 4.3 broadcast.221.clone.1
  228.7 25.8 %scatter_fusion.1 = f32[512,32,128]{2,1,0:T(8,128)} fusion(f32[512,32,128]{2,1,0:T(8,128)} %broadcast.221.clone.1, s32[192]{0:T(256)S(1)} %bitcast.130, f32[192,32,128]{2,1,0:T(8,128)} %fusion.9), kind=kCustom, calls=%fused_computation.7 | custom fusion | flops 786432 | bytes 9437952 | tf_op jit(solution)/shard_map/scatter-add | solution.py:67
  254.6 100.3 %reduce-scatter.6.cloned.1.call-done = f32[16,32,128]{2,1,0:T(8,128)} async-done(((f32[512,32,128]{2,1,0:T(8,128)}), f32[16,32,128]{2,1,0:T(8,128)}) %reduce-scatter.6.cloned.1.call-update) | async-done | bytes 262160 | tf_op jit(solution)/shard_map/reduce_scatter | solution.py:68
  354.9 2.7 convolution_add_fusion.1
  357.7 1.6 collective-permute-start.14
  359.3 4.7 collective-permute-done.14
  364.7 2.5 collective-permute-start.18
  367.2 3.4 collective-permute-done.15
  370.8 3.3 collective-permute-start.19
  374.2 3.9 collective-permute-done.16
  378.0 3.2 collective-permute-start.20
  381.3 2.9 collective-permute-done.17
  384.4 1.0 copy-done.3
  385.4 2.0 gather_fusion.4
  387.4 2.0 gather_fusion.5
  389.4 8.4 %fusion.12 = f32[192,32,128]{2,1,0:T(8,128)} fusion(bf16[192,32,128]{2,1,0:T(8,128)(2,1)} %gather_fusion.5, bf16[1,1,192,128,128]{4,3,2,1,0:T(8,128)(2,1)} %param.6, pred[192]{0:T(512)(128)(4,1)S(1)} %iota_compare_fusion), kind=kOutput, calls=%fused_computation.17 | convolution fusion | flops 202113024 | bytes 11010240 | tf_op jit(solution)/shard_map/ski,soi->sko/dot_general | solution.py:46
  397.8 4.3 broadcast.221
  402.1 25.8 %scatter_fusion.2 = f32[512,32,128]{2,1,0:T(8,128)} fusion(f32[512,32,128]{2,1,0:T(8,128)} %broadcast.221, s32[192]{0:T(256)S(1)} %bitcast.131, f32[192,32,128]{2,1,0:T(8,128)} %fusion.12), kind=kCustom, calls=%fused_computation.8 | custom fusion | flops 786432 | bytes 9437952 | tf_op jit(solution)/shard_map/scatter-add | solution.py:67
  428.0 100.3 %reduce-scatter.8.cloned.1.call-done = f32[16,32,128]{2,1,0:T(8,128)} async-done(((f32[512,32,128]{2,1,0:T(8,128)}), f32[16,32,128]{2,1,0:T(8,128)}) %reduce-scatter.8.cloned.1.call-update) | async-done | bytes 262160 | tf_op jit(solution)/shard_map/reduce_scatter | solution.py:68
  528.3 3.4 fusion.15
  (63 shorter events, 5.2 us)
Async XLA Ops:
  6.5 1.2 copy-start
  6.5 174.9 %reduce-scatter.4.cloned.1.call-start = ((), (), s32[]{:S(2)}) async-start(), calls=%async_computation.3 | async-start | bytes 8650752 | tf_op jit(solution)/shard_map/reduce_scatter | solution.py:68
  10.5 9.4 %collective-permute-start = (bf16[1,16,32,128]{3,2,1,0:T(8,128)(2,1)S(1)}, bf16[1,16,32,128]{3,2,1,0:T(8,128)(2,1)S(1)}, u32[]{:S(2)}, u32[]{:S(2)}) collective-permute-start(bf16[1,16,32,128]{3,2,1,0:T(8,128)(2,1)S(1)} %convert_bitcast_fusion.2), channel_id=1, source_target_pairs={{0,1},{1,2},{2,3},{3,4},{4,5},{5,6},{6,7},{7,0},{8,9},{9,10},{10,1... | collective-permute-start | bytes 393224 | tf_op jit(solution)/shard_map/ppermute | solution.py:24
  12.5 14.3 %collective-permute-start.4 = (bf16[1,16,32,128]{3,2,1,0:T(8,128)(2,1)S(1)}, bf16[1,16,32,128]{3,2,1,0:T(8,128)(2,1)S(1)}, u32[]{:S(2)}, u32[]{:S(2)}) collective-permute-start(bf16[1,16,32,128]{3,2,1,0:T(8,128)(2,1)S(1)} %convert_bitcast_fusion.2), channel_id=1, source_target_pairs={{1,0},{2,1},{3,2},{4,3},{5,4},{6,5},{7,6},{0,7},{9,8},{10,9},{11,1... | collective-permute-start | bytes 393224 | tf_op jit(solution)/shard_map/ppermute | solution.py:27
  19.9 6.2 %collective-permute-start.1 = (bf16[1,16,32,128]{3,2,1,0:T(8,128)(2,1)S(1)}, bf16[1,16,32,128]{3,2,1,0:T(8,128)(2,1)S(1)}, u32[]{:S(2)}, u32[]{:S(2)}) collective-permute-start(bf16[1,16,32,128]{3,2,1,0:T(8,128)(2,1)S(1)} %collective-permute-done), channel_id=1, source_target_pairs={{0,1},{1,2},{2,3},{3,4},{4,5},{5,6},{6,7},{7,0},{8,9},{9,10},{10,1... | collective-permute-start | bytes 393224 | tf_op jit(solution)/shard_map/ppermute | solution.py:24
  26.1 6.2 %collective-permute-start.2 = (bf16[1,16,32,128]{3,2,1,0:T(8,128)(2,1)S(1)}, bf16[1,16,32,128]{3,2,1,0:T(8,128)(2,1)S(1)}, u32[]{:S(2)}, u32[]{:S(2)}) collective-permute-start(bf16[1,16,32,128]{3,2,1,0:T(8,128)(2,1)S(1)} %collective-permute-done.1), channel_id=1, source_target_pairs={{0,1},{1,2},{2,3},{3,4},{4,5},{5,6},{6,7},{7,0},{8,9},{9,10},{10,1... | collective-permute-start | bytes 393224 | tf_op jit(solution)/shard_map/ppermute | solution.py:24
  26.8 5.8 %collective-permute-start.5 = (bf16[1,16,32,128]{3,2,1,0:T(8,128)(2,1)S(1)}, bf16[1,16,32,128]{3,2,1,0:T(8,128)(2,1)S(1)}, u32[]{:S(2)}, u32[]{:S(2)}) collective-permute-start(bf16[1,16,32,128]{3,2,1,0:T(8,128)(2,1)S(1)} %collective-permute-done.4), channel_id=1, source_target_pairs={{1,0},{2,1},{3,2},{4,3},{5,4},{6,5},{7,6},{0,7},{9,8},{10,9},{11,1... | collective-permute-start | bytes 393224 | tf_op jit(solution)/shard_map/ppermute | solution.py:27
  32.3 6.2 %collective-permute-start.3 = (bf16[1,16,32,128]{3,2,1,0:T(8,128)(2,1)S(1)}, bf16[1,16,32,128]{3,2,1,0:T(8,128)(2,1)S(1)}, u32[]{:S(2)}, u32[]{:S(2)}) collective-permute-start(bf16[1,16,32,128]{3,2,1,0:T(8,128)(2,1)S(1)} %collective-permute-done.2), channel_id=1, source_target_pairs={{0,1},{1,2},{2,3},{3,4},{4,5},{5,6},{6,7},{7,0},{8,9},{9,10},{10,1... | collective-permute-start | bytes 393224 | tf_op jit(solution)/shard_map/ppermute | solution.py:24
  32.6 6.2 %collective-permute-start.6 = (bf16[1,16,32,128]{3,2,1,0:T(8,128)(2,1)S(1)}, bf16[1,16,32,128]{3,2,1,0:T(8,128)(2,1)S(1)}, u32[]{:S(2)}, u32[]{:S(2)}) collective-permute-start(bf16[1,16,32,128]{3,2,1,0:T(8,128)(2,1)S(1)} %collective-permute-done.5), channel_id=1, source_target_pairs={{1,0},{2,1},{3,2},{4,3},{5,4},{6,5},{7,6},{0,7},{9,8},{10,9},{11,1... | collective-permute-start | bytes 393224 | tf_op jit(solution)/shard_map/ppermute | solution.py:27
  80.1 101.3 %copy-start.1 = (f32[1,16,32,128]{3,2,1,0:T(8,128)S(1)}, f32[1,16,32,128]{3,2,1,0:T(8,128)}, u32[]{:S(2)}) copy-start(f32[1,16,32,128]{3,2,1,0:T(8,128)} %param.11) | copy-start | bytes 786436
  80.1 274.8 %reduce-scatter.6.cloned.1.call-start = ((), (), s32[]{:S(2)}) async-start(), calls=%async_computation.4 | async-start | bytes 8650752 | tf_op jit(solution)/shard_map/reduce_scatter | solution.py:68
  184.1 6.5 %collective-permute-start.7 = (bf16[1,16,32,128]{3,2,1,0:T(8,128)(2,1)S(1)}, bf16[1,16,32,128]{3,2,1,0:T(8,128)(2,1)S(1)}, u32[]{:S(2)}, u32[]{:S(2)}) collective-permute-start(bf16[1,16,32,128]{3,2,1,0:T(8,128)(2,1)S(1)} %convert_bitcast_fusion.1), channel_id=1, source_target_pairs={{0,1},{1,2},{2,3},{3,4},{4,5},{5,6},{6,7},{7,0},{8,9},{9,10},{10,1... | collective-permute-start | bytes 393224 | tf_op jit(solution)/shard_map/ppermute | solution.py:24
  190.6 6.6 %collective-permute-start.8 = (bf16[1,16,32,128]{3,2,1,0:T(8,128)(2,1)S(1)}, bf16[1,16,32,128]{3,2,1,0:T(8,128)(2,1)S(1)}, u32[]{:S(2)}, u32[]{:S(2)}) collective-permute-start(bf16[1,16,32,128]{3,2,1,0:T(8,128)(2,1)S(1)} %collective-permute-done.7), channel_id=1, source_target_pairs={{0,1},{1,2},{2,3},{3,4},{4,5},{5,6},{6,7},{7,0},{8,9},{9,10},{10,1... | collective-permute-start | bytes 393224 | tf_op jit(solution)/shard_map/ppermute | solution.py:24
  191.3 6.1 %collective-permute-start.11 = (bf16[1,16,32,128]{3,2,1,0:T(8,128)(2,1)S(1)}, bf16[1,16,32,128]{3,2,1,0:T(8,128)(2,1)S(1)}, u32[]{:S(2)}, u32[]{:S(2)}) collective-permute-start(bf16[1,16,32,128]{3,2,1,0:T(8,128)(2,1)S(1)} %convert_bitcast_fusion.1), channel_id=1, source_target_pairs={{1,0},{2,1},{3,2},{4,3},{5,4},{6,5},{7,6},{0,7},{9,8},{10,9},{11,1... | collective-permute-start | bytes 393224 | tf_op jit(solution)/shard_map/ppermute | solution.py:27
  197.2 7.4 %collective-permute-start.9 = (bf16[1,16,32,128]{3,2,1,0:T(8,128)(2,1)S(1)}, bf16[1,16,32,128]{3,2,1,0:T(8,128)(2,1)S(1)}, u32[]{:S(2)}, u32[]{:S(2)}) collective-permute-start(bf16[1,16,32,128]{3,2,1,0:T(8,128)(2,1)S(1)} %collective-permute-done.8), channel_id=1, source_target_pairs={{0,1},{1,2},{2,3},{3,4},{4,5},{5,6},{6,7},{7,0},{8,9},{9,10},{10,1... | collective-permute-start | bytes 393224 | tf_op jit(solution)/shard_map/ppermute | solution.py:24
  197.4 7.2 %collective-permute-start.12 = (bf16[1,16,32,128]{3,2,1,0:T(8,128)(2,1)S(1)}, bf16[1,16,32,128]{3,2,1,0:T(8,128)(2,1)S(1)}, u32[]{:S(2)}, u32[]{:S(2)}) collective-permute-start(bf16[1,16,32,128]{3,2,1,0:T(8,128)(2,1)S(1)} %collective-permute-done.11), channel_id=1, source_target_pairs={{1,0},{2,1},{3,2},{4,3},{5,4},{6,5},{7,6},{0,7},{9,8},{10,9},{11,1... | collective-permute-start | bytes 393224 | tf_op jit(solution)/shard_map/ppermute | solution.py:27
  204.6 6.2 %collective-permute-start.10 = (bf16[1,16,32,128]{3,2,1,0:T(8,128)(2,1)S(1)}, bf16[1,16,32,128]{3,2,1,0:T(8,128)(2,1)S(1)}, u32[]{:S(2)}, u32[]{:S(2)}) collective-permute-start(bf16[1,16,32,128]{3,2,1,0:T(8,128)(2,1)S(1)} %collective-permute-done.9), channel_id=1, source_target_pairs={{0,1},{1,2},{2,3},{3,4},{4,5},{5,6},{6,7},{7,0},{8,9},{9,10},{10,1... | collective-permute-start | bytes 393224 | tf_op jit(solution)/shard_map/ppermute | solution.py:24
  204.6 6.4 %collective-permute-start.13 = (bf16[1,16,32,128]{3,2,1,0:T(8,128)(2,1)S(1)}, bf16[1,16,32,128]{3,2,1,0:T(8,128)(2,1)S(1)}, u32[]{:S(2)}, u32[]{:S(2)}) collective-permute-start(bf16[1,16,32,128]{3,2,1,0:T(8,128)(2,1)S(1)} %collective-permute-done.12), channel_id=1, source_target_pairs={{1,0},{2,1},{3,2},{4,3},{5,4},{6,5},{7,6},{0,7},{9,8},{10,9},{11,1... | collective-permute-start | bytes 393224 | tf_op jit(solution)/shard_map/ppermute | solution.py:27
  211.0 1.0 copy-start.2
  254.6 273.7 %reduce-scatter.8.cloned.1.call-start = ((), (), s32[]{:S(2)}) async-start(), calls=%async_computation.5 | async-start | bytes 8650752 | tf_op jit(solution)/shard_map/reduce_scatter | solution.py:68
  357.7 6.3 %collective-permute-start.14 = (bf16[1,16,32,128]{3,2,1,0:T(8,128)(2,1)S(1)}, bf16[1,16,32,128]{3,2,1,0:T(8,128)(2,1)S(1)}, u32[]{:S(2)}, u32[]{:S(2)}) collective-permute-start(bf16[1,16,32,128]{3,2,1,0:T(8,128)(2,1)S(1)} %convert_bitcast_fusion), channel_id=1, source_target_pairs={{0,1},{1,2},{2,3},{3,4},{4,5},{5,6},{6,7},{7,0},{8,9},{9,10},{10,1... | collective-permute-start | bytes 393224 | tf_op jit(solution)/shard_map/ppermute | solution.py:24
  364.0 6.6 %collective-permute-start.15 = (bf16[1,16,32,128]{3,2,1,0:T(8,128)(2,1)S(1)}, bf16[1,16,32,128]{3,2,1,0:T(8,128)(2,1)S(1)}, u32[]{:S(2)}, u32[]{:S(2)}) collective-permute-start(bf16[1,16,32,128]{3,2,1,0:T(8,128)(2,1)S(1)} %collective-permute-done.14), channel_id=1, source_target_pairs={{0,1},{1,2},{2,3},{3,4},{4,5},{5,6},{6,7},{7,0},{8,9},{9,10},{10,1... | collective-permute-start | bytes 393224 | tf_op jit(solution)/shard_map/ppermute | solution.py:24
  364.7 6.1 %collective-permute-start.18 = (bf16[1,16,32,128]{3,2,1,0:T(8,128)(2,1)S(1)}, bf16[1,16,32,128]{3,2,1,0:T(8,128)(2,1)S(1)}, u32[]{:S(2)}, u32[]{:S(2)}) collective-permute-start(bf16[1,16,32,128]{3,2,1,0:T(8,128)(2,1)S(1)} %convert_bitcast_fusion), channel_id=1, source_target_pairs={{1,0},{2,1},{3,2},{4,3},{5,4},{6,5},{7,6},{0,7},{9,8},{10,9},{11,1... | collective-permute-start | bytes 393224 | tf_op jit(solution)/shard_map/ppermute | solution.py:27
  370.6 7.4 %collective-permute-start.16 = (bf16[1,16,32,128]{3,2,1,0:T(8,128)(2,1)S(1)}, bf16[1,16,32,128]{3,2,1,0:T(8,128)(2,1)S(1)}, u32[]{:S(2)}, u32[]{:S(2)}) collective-permute-start(bf16[1,16,32,128]{3,2,1,0:T(8,128)(2,1)S(1)} %collective-permute-done.15), channel_id=1, source_target_pairs={{0,1},{1,2},{2,3},{3,4},{4,5},{5,6},{6,7},{7,0},{8,9},{9,10},{10,1... | collective-permute-start | bytes 393224 | tf_op jit(solution)/shard_map/ppermute | solution.py:24
  370.8 7.2 %collective-permute-start.19 = (bf16[1,16,32,128]{3,2,1,0:T(8,128)(2,1)S(1)}, bf16[1,16,32,128]{3,2,1,0:T(8,128)(2,1)S(1)}, u32[]{:S(2)}, u32[]{:S(2)}) collective-permute-start(bf16[1,16,32,128]{3,2,1,0:T(8,128)(2,1)S(1)} %collective-permute-done.18), channel_id=1, source_target_pairs={{1,0},{2,1},{3,2},{4,3},{5,4},{6,5},{7,6},{0,7},{9,8},{10,9},{11,1... | collective-permute-start | bytes 393224 | tf_op jit(solution)/shard_map/ppermute | solution.py:27
  378.0 6.2 %collective-permute-start.17 = (bf16[1,16,32,128]{3,2,1,0:T(8,128)(2,1)S(1)}, bf16[1,16,32,128]{3,2,1,0:T(8,128)(2,1)S(1)}, u32[]{:S(2)}, u32[]{:S(2)}) collective-permute-start(bf16[1,16,32,128]{3,2,1,0:T(8,128)(2,1)S(1)} %collective-permute-done.16), channel_id=1, source_target_pairs={{0,1},{1,2},{2,3},{3,4},{4,5},{5,6},{6,7},{7,0},{8,9},{9,10},{10,1... | collective-permute-start | bytes 393224 | tf_op jit(solution)/shard_map/ppermute | solution.py:24
  378.0 6.4 %collective-permute-start.20 = (bf16[1,16,32,128]{3,2,1,0:T(8,128)(2,1)S(1)}, bf16[1,16,32,128]{3,2,1,0:T(8,128)(2,1)S(1)}, u32[]{:S(2)}, u32[]{:S(2)}) collective-permute-start(bf16[1,16,32,128]{3,2,1,0:T(8,128)(2,1)S(1)} %collective-permute-done.19), channel_id=1, source_target_pairs={{1,0},{2,1},{3,2},{4,3},{5,4},{6,5},{7,6},{0,7},{9,8},{10,9},{11,1... | collective-permute-start | bytes 393224 | tf_op jit(solution)/shard_map/ppermute | solution.py:27
  384.4 1.0 copy-start.3
Sparse Core Ops, SparseCore 0:
  80.3 101.0 reduce-scatter.3
  254.7 100.1 reduce-scatter.5
  428.1 100.1 reduce-scatter.7
